TPU v7x, 32 devices: a whole 2x2x4 slice. The times are simulated.
32 devices in a mesh: groups: 2 (over y), latent: 8 (over z, x), hidden: 2 (over core).
Axes of the slice: x: 2, y: 2, z: 4, core: 2. Of those that a mesh axis runs over, the one named last changes fastest.
Arguments:
- input_codes: int32 [288, 2304], P('groups', ('latent', 'hidden')), parts along dimension 0, may hold values from -128 to 127
- cotangent_codes: int32 [288, 2304], P('groups', ('latent', 'hidden')), parts along dimension 0, may hold values from -128 to 127
- dictionary: bfloat16 [8192, 2304], P(('latent', 'hidden')), as said below
- encoder_bias: float32 [8192], P(('latent', 'hidden')), may hold values from -12 to 0, as said below
- decoder_bias: float32 [2304], replicated, may hold values from -1.2 to 1.2
- norm_gain: float32 [2304], replicated, may hold values from 0.1 to 1.9
- gate_weight: bfloat16 [8192, 2304], P(('latent', 'hidden')), may hold values from -0.1875 to 0.1875
- up_weight: bfloat16 [8192, 2304], P(('latent', 'hidden')), may hold values from -0.1875 to 0.1875
- down_weight: bfloat16 [8192, 2304], P(('latent', 'hidden')), may hold values from -0.09375 to 0.09375
Outputs:
- block_output: bfloat16 [288, 2304], P('groups', ('latent', 'hidden')), parts along dimension 0
- dictionary_grad: bfloat16 [8192, 4608], P(('latent', 'hidden'), 'groups'), parts along dimension 1
There are 2 independent parts, one for each index of `groups`. A program takes and returns all parts, laid end to end along the dimension named above; an argument that names none is the same for every part. Nothing has to cross between parts.
Inputs may be any that keep to these rules, and one draw needn't show every extreme that they name: `dictionary`: every entry is a whole multiple of 2^-10, at most 119 such units in magnitude. `encoder_bias`: every entry is a whole multiple of 2^-16.
All inputs are finite; a program needn't handle non-finite values.
Results may differ from a plain program's by a relative error of at most 0.0072.
Values may be sent and summed in bfloat16 or wider, within the bound.
A program may use at most 64 MiB of HBM per device.

v0:
```python
import jax
import jax.numpy as jnp
from jax import lax
from jax.sharding import PartitionSpec as P

CODE_STEP = 2.0 ** (-6)
NORM_EPSILON = 1e-06
GELU_ROOT = 0.7978845608028654
GELU_CUBIC = 0.044715
ACROSS = (((1,), (1,)), ((), ()))
DOWNWARD = (((0,), (0,)), ((), ()))


def gelu_parts(values):
    argument = GELU_ROOT * (values + GELU_CUBIC * values * values * values)
    tanh_value = jnp.tanh(argument)
    result = 0.5 * values * (1.0 + tanh_value)
    derivative = 0.5 * (1.0 + tanh_value) + 0.5 * values * (
        1.0 - tanh_value * tanh_value
    ) * GELU_ROOT * (1.0 + 3.0 * GELU_CUBIC * values * values)
    return (result, derivative)


def per_device(
    input_codes,
    cotangent_codes,
    dictionary,
    encoder_bias,
    decoder_bias,
    norm_gain,
    gate_weight,
    up_weight,
    down_weight,
):
    own_width = input_codes.shape[1]
    model_width = own_width * lax.axis_size(("latent", "hidden"))
    cotangent_local = (cotangent_codes.astype(jnp.float32) * CODE_STEP).astype(jnp.bfloat16)
    hidden_grad = None
    inputs_local = (input_codes.astype(jnp.float32) * CODE_STEP).astype(jnp.bfloat16)
    inputs = lax.all_gather(inputs_local, ("latent", "hidden"), axis=1, tiled=True)
    preact = (
        lax.dot_general(inputs, dictionary, ACROSS, preferred_element_type=jnp.float32)
        + encoder_bias
    )
    latents = jnp.maximum(preact, 0.0).astype(jnp.bfloat16)
    partial_value = jnp.dot(latents, dictionary, preferred_element_type=jnp.float32)
    rebuilt = lax.psum(partial_value, ("latent", "hidden")) + decoder_bias
    inverse = lax.rsqrt(
        jnp.sum(rebuilt * rebuilt, axis=1, keepdims=True) / model_width + NORM_EPSILON
    )
    normed = (rebuilt * inverse * norm_gain).astype(jnp.bfloat16)
    target = inputs.astype(jnp.float32)
    gate_proj = lax.dot_general(normed, gate_weight, ACROSS, preferred_element_type=jnp.float32)
    up_proj = lax.dot_general(normed, up_weight, ACROSS, preferred_element_type=jnp.float32)
    gelu_value, gelu_slope = gelu_parts(gate_proj)
    hidden = (gelu_value * up_proj).astype(jnp.bfloat16)
    output_terms = jnp.dot(hidden, down_weight, preferred_element_type=jnp.float32)
    block_output = lax.psum_scatter(
        output_terms, ("latent", "hidden"), scatter_dimension=1, tiled=True
    ).astype(jnp.bfloat16)
    hidden_grad = lax.dot_general(
        lax.all_gather(cotangent_local, ("latent", "hidden"), axis=1, tiled=True),
        down_weight,
        ACROSS,
        preferred_element_type=jnp.float32,
    )
    gate_grad = (hidden_grad * up_proj * gelu_slope).astype(jnp.bfloat16)
    up_grad = (hidden_grad * gelu_value).astype(jnp.bfloat16)
    partial_grad = jnp.dot(gate_grad, gate_weight, preferred_element_type=jnp.float32) + jnp.dot(
        up_grad, up_weight, preferred_element_type=jnp.float32
    )
    scaled = lax.psum(partial_grad, ("latent", "hidden")) * norm_gain
    inner_row = jnp.sum(scaled * rebuilt, axis=1, keepdims=True)
    inverse_cube = inverse * inverse * inverse
    rebuilt_grad = (
        inverse * scaled - inverse_cube * rebuilt * (inner_row / model_width) + (rebuilt - target)
    ).astype(jnp.bfloat16)
    latent_grad = lax.dot_general(
        rebuilt_grad, dictionary, ACROSS, preferred_element_type=jnp.float32
    )
    preact_grad = jnp.where(preact > 0.0, latent_grad, 0.0).astype(jnp.bfloat16)
    dictionary_grad = lax.dot_general(
        latents, rebuilt_grad, DOWNWARD, preferred_element_type=jnp.float32
    ) + lax.dot_general(preact_grad, inputs, DOWNWARD, preferred_element_type=jnp.float32)
    return (block_output, dictionary_grad.astype(jnp.bfloat16))


def solution(mesh):
    in_specs = (
        P("groups", ("latent", "hidden")),
        P("groups", ("latent", "hidden")),
        P(("latent", "hidden"), None),
        P(("latent", "hidden")),
        P(),
        P(),
        P(("latent", "hidden"), None),
        P(("latent", "hidden"), None),
        P(("latent", "hidden"), None),
    )
    out_specs = (P("groups", ("latent", "hidden")), P(("latent", "hidden"), "groups"))
    return jax.shard_map(
        per_device, mesh=mesh, in_specs=in_specs, out_specs=out_specs, check_vma=False
    )
```

profile of v0, /device:TPU:0, one launch (start us, length us, event | category | flops | bytes accessed | tf_op | source)
XLA Modules:
  0.0 309.8 jit_solution(10657653489420089251)
XLA Ops:
  7.2 0.0 all-reduce.3.cloned.1.call-start
  7.2 1.2 copy.11
  8.4 26.4 %all_gather.6 = bf16[144,2304]{0,1:T(8,128)(2,1)S(1)} all-gather(bf16[144,144]{0,1:T(8,128)(2,1)S(1)} %multiply_convert_fusion.6), channel_id=1, replica_groups=mesh['groups'=2,'latent'=8,'hidden'=2] {'latent','hidden'}, dimensions={1}, use_global_device_ids=true | all-gather | bytes 705024 | tf_op jit(solution)/shard_map/all_gather | solution.py:40
  34.8 0.9 convolution_add_fusion.2
  35.8 0.7 copy-done.8
  36.5 1.6 fusion.19
  38.1 0.0 all-reduce.3.cloned.1.call-update
  38.1 0.0 all-reduce.5.cloned.1.call-start
  38.1 1.7 copy.12
  39.8 0.9 multiply_convert_fusion.5
  40.7 24.5 %all_gather.7 = bf16[144,2304]{0,1:T(8,128)(2,1)S(1)} all-gather(bf16[144,144]{0,1:T(8,128)(2,1)S(1)} %multiply_convert_fusion.5), channel_id=1, replica_groups=mesh['groups'=2,'latent'=8,'hidden'=2] {'latent','hidden'}, dimensions={1}, use_global_device_ids=true | all-gather | bytes 705024 | tf_op jit(solution)/shard_map/all_gather | solution.py:62
  65.3 3.4 %fusion.38 = f32[144,512]{1,0:T(8,128)} fusion(bf16[144,2304]{0,1:T(8,128)(2,1)S(1)} %all_gather.7, bf16[512,2304]{1,0:T(8,128)(2,1)} %param.17), kind=kOutput, calls=%fused_computation.57 | convolution fusion | flops 339738624 | bytes 3317760 | tf_op jit(solution)/shard_map/dot_general | solution.py:61
  68.6 63.1 %all-reduce.3.cloned.1.call-done = f32[144,2304]{1,0:T(8,128)} async-done(((f32[144,2304]{1,0:T(8,128)}), f32[144,2304]{1,0:T(8,128)}) %all-reduce.3.cloned.1.call-update) | async-done | bytes 1327120 | tf_op jit(solution)/shard_map/psum | solution.py:47
  131.7 1.6 multiply_reduce_fusion.1
  133.3 0.6 multiply_multiply_fusion.1
  133.9 2.8 fusion.37
  136.7 0.9 fusion.36
  137.7 0.8 copy-done.3
  138.5 0.7 fusion.11
  139.2 0.1 copy-done.7
  139.2 1.7 convolution_add_fusion.1
  140.9 0.0 reduce-scatter.4.cloned.1.call-start
  141.0 1.3 copy.13
  142.2 4.4 %convolution_bitcast_fusion = f32[2304,144]{1,0:T(8,128)} fusion(bf16[512,2304]{1,0:T(8,128)(2,1)} %param.17, f32[144,512]{1,0:T(8,128)} %copy-done.7, f32[144,512]{1,0:T(8,128)} %copy-done.5), kind=kOutput, calls=%fused_computation.2 | convolution fusion | flops 340475904 | bytes 4276224
  146.6 88.4 %all-reduce.5.cloned.1.call-done = f32[144,2304]{1,0:T(8,128)} async-done(((f32[144,2304]{1,0:T(8,128)}), f32[144,2304]{1,0:T(8,128)}) %all-reduce.5.cloned.1.call-update) | async-done | bytes 1327120 | tf_op jit(solution)/shard_map/psum | solution.py:72
  235.0 2.1 multiply_reduce_fusion
  237.1 0.4 copy-done.6
  237.5 2.5 add_convert_fusion
  240.0 5.1 %fusion.2 = f32[512,2304]{1,0:T(8,128)} fusion(bf16[144,2304]{0,1:T(8,128)(2,1)S(1)} %all_gather.6, bf16[144,2304]{1,0:T(8,128)(2,1)} %add_convert_fusion, bf16[512,2304]{1,0:T(8,128)(2,1)S(1)} %copy-done, f32[144,512]{1,0:T(8,128)} %copy-done.8), kind=kOutput, calls=%fused_computation.11 | convolution fusion | flops 679698432 | bytes 8699904 | tf_op jit(solution)/shard_map/dot_general | solution.py:84
  245.1 5.1 %fusion = bf16[512,2304]{1,0:T(8,128)(2,1)} fusion(f32[512,2304]{1,0:T(8,128)} %fusion.2, bf16[144,2304]{1,0:T(8,128)(2,1)} %add_convert_fusion, f32[144,512]{1,0:T(8,128)} %copy-done.8), kind=kOutput, calls=%fused_computation.1 | convolution fusion | flops 342245376 | bytes 8036352 | tf_op jit(solution)/shard_map/dot_general | solution.py:82
  250.2 51.5 %reduce-scatter.4.cloned.1.call-done = f32[144,144]{1,0:T(8,128)} async-done(((f32[2304,144]{1,0:T(8,128)}), f32[144,144]{1,0:T(8,128)}) %reduce-scatter.4.cloned.1.call-update) | async-done | bytes 82960
  301.7 1.6 copy.15
  (30 shorter events, 0.1 us)
Async XLA Ops:
  7.2 27.7 %copy-start = (bf16[512,2304]{1,0:T(8,128)(2,1)S(1)}, bf16[512,2304]{1,0:T(8,128)(2,1)}, u32[]{:S(2)}) copy-start(bf16[512,2304]{1,0:T(8,128)(2,1)} %param.11) | copy-start | bytes 7077892
  7.2 27.7 %copy-start.14 = (f32[512]{0:T(512)S(1)}, f32[512]{0:T(512)}, u32[]{:S(2)}) copy-start(f32[512]{0:T(512)} %param.12) | copy-start | bytes 6148
  7.2 124.5 %all-reduce.3.cloned.1.call-start = ((), (), s32[]{:S(2)}) async-start(), calls=%async_computation.1 | async-start | bytes 2654208 | tf_op jit(solution)/shard_map/psum | solution.py:47
  35.8 0.7 copy-start.8
  38.1 196.9 %all-reduce.5.cloned.1.call-start = ((), (), s32[]{:S(2)}) async-start(), calls=%async_computation.2 | async-start | bytes 2654208 | tf_op jit(solution)/shard_map/psum | solution.py:72
  65.3 66.4 %copy-start.10 = (f32[2304]{0:T(1024)S(1)}, f32[2304]{0:T(1024)}, u32[]{:S(2)}) copy-start(f32[2304]{0:T(1024)} %param.13) | copy-start | bytes 27652
  131.7 2.2 copy-start.1
  131.7 2.2 copy-start.11
  133.9 2.8 copy-start.4
  136.7 2.5 copy-start.5
  136.7 1.8 copy-start.3
  136.7 1.8 copy-start.9
  138.5 0.7 copy-start.7
  140.9 160.8 %reduce-scatter.4.cloned.1.call-start = ((), (), s32[]{:S(2)}) async-start(), calls=%async_computation.3 | async-start | bytes 2506752
  235.0 2.2 copy-start.2
  235.0 2.5 copy-start.6
  235.0 2.5 copy-start.12
  235.0 2.5 copy-start.13
Sparse Core Ops, SparseCore 0:
  38.2 93.4 all-reduce.2
  141.0 93.9 all-reduce.4
  238.7 62.8 reduce-scatter.3
where the time goes:
time: 310 us
  waiting for transfers between devices  203 us (65%)
  blocking collectives  50.9 us (16%)
  matrix products  26.4 us (9%)
  between operations  13.9 us (4%)
  other arithmetic  7.82 us (3%)
  local copies, waits for them, and re-layouts  7.76 us (3%)
    psum x1, waiting for transfers between devices, per_device(): scaled = lax.psum(partial_grad, ('latent', 'hidden')) * norm_gain  88.4 us
    psum x1, waiting for transfers between devices, per_device(): rebuilt = lax.psum(partial_value, ('latent', 'hidden')) + decoder_bias  63.1 us
    unnamed x4, waiting for transfers between devices  51.5 us
    all_gather x1, blocking collectives, per_device(): lax.all_gather(inputs_local, ('latent', 'hidden'), axis=1, tiled=True)  26.4 us
    all_gather x1, blocking collectives, per_device(): lax.all_gather(cotangent_local, ('latent', 'hidden'), axis=1, tiled=True)  24.5 us
    unnamed x33, local copies, waits for them, and re-layouts  6.49 us
  transfers between devices with their start and end apart: 3, of which 3 were waited for; matrix products, arithmetic and copies ran while one was open for 9% of the time, Pallas kernels for 0%

commit v1 on v0

--- a/solution.py
+++ b/solution.py
@@ -44,7 +44,7 @@
     )
     latents = jnp.maximum(preact, 0.0).astype(jnp.bfloat16)
     partial_value = jnp.dot(latents, dictionary, preferred_element_type=jnp.float32)
-    rebuilt = lax.psum(partial_value, ("latent", "hidden")) + decoder_bias
+    rebuilt = lax.psum(lax.psum(partial_value, "hidden"), "latent") + decoder_bias
     inverse = lax.rsqrt(
         jnp.sum(rebuilt * rebuilt, axis=1, keepdims=True) / model_width + NORM_EPSILON
     )

time: 310 us -> 327 us (1.055)
  waiting for transfers between devices: 203 us -> 214 us
  blocking collectives: 50.9 us -> 56.1 us
    psum x1 -> x2, waiting for transfers between devices: 63.1 us -> 74.9 us  [the longest x1 57.6 us: per_device(): lax.psum(lax.psum(partial_value, 'hidden'), 'latent') + decoder_bias]
    all_gather x1, blocking collectives: 24.5 us -> 29.7 us  [per_device(): lax.all_gather(cotangent_local, ('latent', 'hidden'), axis=1, tiled=True)]
    unnamed x4 -> x5, waiting for transfers between devices: 51.5 us -> 51.4 us
  transfers between devices with their start and end apart: 3 -> 4, of which waited for: 3 -> 4; matrix products, arithmetic and copies ran while one was open for 9% -> 8% of each run, Pallas kernels for 0% -> 0%
where the time goes in v1:
time: 327 us; the launch traced here: 326 us
  waiting for transfers between devices  214 us (65%)
  blocking collectives  56.1 us (17%)
  matrix products  26.4 us (8%)
  between operations  13.9 us (4%)
  other arithmetic  7.82 us (2%)
  local copies, waits for them, and re-layouts  7.76 us (2%)
    psum x1, waiting for transfers between devices, per_device(): scaled = lax.psum(partial_grad, ('latent', 'hidden')) * norm_gain  87.8 us
    psum x1, waiting for transfers between devices, per_device(): lax.psum(lax.psum(partial_value, 'hidden'), 'latent') + decoder_bias  57.6 us
    unnamed x5, waiting for transfers between devices  51.4 us
    all_gather x1, blocking collectives, per_device(): lax.all_gather(cotangent_local, ('latent', 'hidden'), axis=1, tiled=True)  29.7 us
    all_gather x1, blocking collectives, per_device(): lax.all_gather(inputs_local, ('latent', 'hidden'), axis=1, tiled=True)  26.4 us
    psum x1, waiting for transfers between devices, per_device(): lax.psum(partial_value, 'hidden')  17.3 us
  transfers between devices with their start and end apart: 4, of which 4 were waited for; matrix products, arithmetic and copies ran while one was open for 8% of the time, Pallas kernels for 0%

profile of v1, /device:TPU:0, one launch (start us, length us, event | category | flops | bytes accessed | tf_op | source)
XLA Modules:
  0.0 326.2 jit_solution(9593347624886633719)
XLA Ops:
  7.2 1.2 copy.11
  8.4 26.4 %all_gather.6 = bf16[144,2304]{0,1:T(8,128)(2,1)S(1)} all-gather(bf16[144,144]{0,1:T(8,128)(2,1)S(1)} %multiply_convert_fusion.6), channel_id=1, replica_groups=mesh['groups'=2,'latent'=8,'hidden'=2] {'latent','hidden'}, dimensions={1}, use_global_device_ids=true | all-gather | bytes 705024 | tf_op jit(solution)/shard_map/all_gather | solution.py:40
  34.8 0.9 convolution_add_fusion.2
  35.8 0.7 copy-done.8
  36.5 1.6 fusion.19
  38.1 0.0 all-reduce.6.cloned.1.call-start
  38.1 17.3 %all-reduce.4.cloned.1.call-done = f32[144,2304]{1,0:T(8,128)} async-done(((f32[144,2304]{1,0:T(8,128)}), f32[144,2304]{1,0:T(8,128)}) %all-reduce.4.cloned.1.call-update) | async-done | bytes 1327120 | tf_op jit(solution)/shard_map/psum | solution.py:47
  55.5 0.0 all-reduce.8.cloned.1.call-start
  55.5 1.7 copy.12
  57.2 0.9 multiply_convert_fusion.5
  58.1 29.7 %all_gather.7 = bf16[144,2304]{0,1:T(8,128)(2,1)S(1)} all-gather(bf16[144,144]{0,1:T(8,128)(2,1)S(1)} %multiply_convert_fusion.5), channel_id=1, replica_groups=mesh['groups'=2,'latent'=8,'hidden'=2] {'latent','hidden'}, dimensions={1}, use_global_device_ids=true | all-gather | bytes 705024 | tf_op jit(solution)/shard_map/all_gather | solution.py:62
  87.8 3.4 %fusion.38 = f32[144,512]{1,0:T(8,128)} fusion(bf16[144,2304]{0,1:T(8,128)(2,1)S(1)} %all_gather.7, bf16[512,2304]{1,0:T(8,128)(2,1)} %param.17), kind=kOutput, calls=%fused_computation.57 | convolution fusion | flops 339738624 | bytes 3317760 | tf_op jit(solution)/shard_map/dot_general | solution.py:61
  91.2 57.6 %all-reduce.6.cloned.1.call-done = f32[144,2304]{1,0:T(8,128)} async-done(((f32[144,2304]{1,0:T(8,128)}), f32[144,2304]{1,0:T(8,128)}) %all-reduce.6.cloned.1.call-update) | async-done | bytes 1327120 | tf_op jit(solution)/shard_map/psum | solution.py:47
  148.8 1.6 multiply_reduce_fusion.1
  150.4 0.6 multiply_multiply_fusion.1
  151.0 2.8 fusion.37
  153.8 0.9 fusion.36
  154.7 0.8 copy-done.3
  155.6 0.7 fusion.11
  156.2 0.0 copy-done.7
  156.3 1.7 convolution_add_fusion.1
  158.0 0.0 reduce-scatter.4.cloned.1.call-start
  158.0 1.3 copy.13
  159.3 4.4 %convolution_bitcast_fusion = f32[2304,144]{1,0:T(8,128)} fusion(bf16[512,2304]{1,0:T(8,128)(2,1)} %param.17, f32[144,512]{1,0:T(8,128)} %copy-done.7, f32[144,512]{1,0:T(8,128)} %copy-done.5), kind=kOutput, calls=%fused_computation.2 | convolution fusion | flops 340475904 | bytes 4276224
  163.7 87.8 %all-reduce.8.cloned.1.call-done = f32[144,2304]{1,0:T(8,128)} async-done(((f32[144,2304]{1,0:T(8,128)}), f32[144,2304]{1,0:T(8,128)}) %all-reduce.8.cloned.1.call-update) | async-done | bytes 1327120 | tf_op jit(solution)/shard_map/psum | solution.py:72
  251.5 2.1 multiply_reduce_fusion
  253.6 0.4 copy-done.6
  254.0 2.5 add_convert_fusion
  256.5 5.1 %fusion.2 = f32[512,2304]{1,0:T(8,128)} fusion(bf16[144,2304]{0,1:T(8,128)(2,1)S(1)} %all_gather.6, bf16[144,2304]{1,0:T(8,128)(2,1)} %add_convert_fusion, bf16[512,2304]{1,0:T(8,128)(2,1)S(1)} %copy-done, f32[144,512]{1,0:T(8,128)} %copy-done.8), kind=kOutput, calls=%fused_computation.11 | convolution fusion | flops 679698432 | bytes 8699904 | tf_op jit(solution)/shard_map/dot_general | solution.py:84
  261.6 5.1 %fusion = bf16[512,2304]{1,0:T(8,128)(2,1)} fusion(f32[512,2304]{1,0:T(8,128)} %fusion.2, bf16[144,2304]{1,0:T(8,128)(2,1)} %add_convert_fusion, f32[144,512]{1,0:T(8,128)} %copy-done.8), kind=kOutput, calls=%fused_computation.1 | convolution fusion | flops 342245376 | bytes 8036352 | tf_op jit(solution)/shard_map/dot_general | solution.py:82
  266.6 51.3 %reduce-scatter.4.cloned.1.call-done = f32[144,144]{1,0:T(8,128)} async-done(((f32[2304,144]{1,0:T(8,128)}), f32[144,144]{1,0:T(8,128)}) %reduce-scatter.4.cloned.1.call-update) | async-done | bytes 82960
  318.0 1.6 copy.15
  (33 shorter events, 0.2 us)
Async XLA Ops:
  7.2 27.7 %copy-start = (bf16[512,2304]{1,0:T(8,128)(2,1)S(1)}, bf16[512,2304]{1,0:T(8,128)(2,1)}, u32[]{:S(2)}) copy-start(bf16[512,2304]{1,0:T(8,128)(2,1)} %param.11) | copy-start | bytes 7077892
  7.2 27.7 %copy-start.14 = (f32[512]{0:T(512)S(1)}, f32[512]{0:T(512)}, u32[]{:S(2)}) copy-start(f32[512]{0:T(512)} %param.12) | copy-start | bytes 6148
  7.2 48.3 %all-reduce.4.cloned.1.call-start = ((), (), s32[]{:S(2)}) async-start(), calls=%async_computation.1 | async-start | bytes 2654208 | tf_op jit(solution)/shard_map/psum | solution.py:47
  35.8 0.7 copy-start.8
  38.1 110.7 %all-reduce.6.cloned.1.call-start = ((), (), s32[]{:S(2)}) async-start(), calls=%async_computation.2 | async-start | bytes 2654208 | tf_op jit(solution)/shard_map/psum | solution.py:47
  55.5 195.9 %all-reduce.8.cloned.1.call-start = ((), (), s32[]{:S(2)}) async-start(), calls=%async_computation.3 | async-start | bytes 2654208 | tf_op jit(solution)/shard_map/psum | solution.py:72
  87.8 61.0 %copy-start.10 = (f32[2304]{0:T(1024)S(1)}, f32[2304]{0:T(1024)}, u32[]{:S(2)}) copy-start(f32[2304]{0:T(1024)} %param.13) | copy-start | bytes 27652
  148.8 2.2 copy-start.1
  148.8 2.2 copy-start.11
  151.0 2.8 copy-start.4
  153.8 2.5 copy-start.5
  153.8 1.8 copy-start.3
  153.8 1.8 copy-start.9
  155.6 0.7 copy-start.7
  158.0 160.0 %reduce-scatter.4.cloned.1.call-start = ((), (), s32[]{:S(2)}) async-start(), calls=%async_computation.4 | async-start | bytes 2506752
  251.4 2.2 copy-start.2
  251.4 2.5 copy-start.6
  251.4 2.5 copy-start.12
  251.4 2.5 copy-start.13
Sparse Core Ops, SparseCore 0:
  38.2 17.2 all-reduce.3
  59.0 89.7 all-reduce.5
  158.1 93.3 all-reduce.7
  255.1 62.8 reduce-scatter.3
